TPU v7x, 32 devices: a whole 2x2x4 slice. The times are simulated.
32 devices in a mesh: grp: 2 (over y), vec: 4 (over z), walk: 2 (over x), orb: 2 (over core).
Axes of the slice: x: 2, y: 2, z: 4, core: 2. Of those that a mesh axis runs over, the one named last changes fastest.
Arguments:
- walkers: bfloat16 [32, 512, 128], P(('grp', 'walk'), 'orb'), parts along dimension 0, may hold values from -3 to 3
- inv_intersection: bfloat16 [32, 128, 128], P(('grp', 'walk')), parts along dimension 0, may hold values from -0.5 to 0.5
- trial: bfloat16 [512, 128], replicated, may hold values from -0.25 to 0.25
- vectors: bfloat16 [32, 512, 512], P('vec', 'orb')
- aux_field: float32 [32, 32], P(('grp', 'walk'), 'vec'), parts along dimension 0, may hold values from -5 to 5
- log_weight: float32 [32], P(('grp', 'walk')), parts along dimension 0, may hold values from -4 to 4
- copy_list: int32 [32], P(('grp', 'walk')), parts along dimension 0, may hold values from 0 to 15
Outputs:
- walkers_out: bfloat16 [32, 512, 128], P(('grp', 'walk'), 'orb'), parts along dimension 0
- weights_out: float32 [32], P(('grp', 'walk')), parts along dimension 0
There are 2 independent parts, one for each index of `grp`. A program takes and returns all parts, laid end to end along the dimension named above; an argument that names none is the same for every part. Nothing has to cross between parts.
Inputs may be any that keep to these rules, and one draw needn't show every extreme that they name: `copy_list`: the walker, within the same ensemble, whose copy fills the slot.
All inputs are finite; a program needn't handle non-finite values.
Results may differ from a plain program's by a relative error of at most 0.008.
Values may be sent and summed in bfloat16 or wider, within the bound.
No kernel may reach another device: no remote copies, remote signals or barrier semaphores. Data moves between devices by JAX's collectives and lax.ppermute only.
A program may use at most 64 MiB of HBM per device.

v0:
```python
from functools import partial
import math
import jax
import jax.numpy as jnp
from jax import lax
from jax.sharding import PartitionSpec as P

ORDER = 6
step_root = math.sqrt(0.08)


def fold_rows(operator, carry, piece, start):
    return jnp.einsum("wnm,wme->wne", operator, piece, preferred_element_type=jnp.float32)


def per_device(walkers, inv_intersection, trial, vectors, aux_field, log_weight, copy_list):
    green = jnp.einsum(
        "wne,wef->wnf", walkers, inv_intersection, preferred_element_type=jnp.float32
    ).astype(jnp.bfloat16)
    mixed = jnp.einsum("gnm,me->gne", vectors, trial, preferred_element_type=jnp.float32).astype(
        jnp.bfloat16
    )
    partial_bias = jnp.einsum("wne,gne->wg", green, mixed, preferred_element_type=jnp.float32)
    bias = lax.psum(partial_bias, "orb")
    shift = -step_root * bias
    field = aux_field - shift
    own_factor = jnp.sum(aux_field * shift - 0.5 * shift * shift, axis=1)
    new_log = log_weight + lax.psum(own_factor, "vec")
    weighted = (field * step_root).astype(jnp.bfloat16)
    local_operator = jnp.einsum(
        "wg,gnm->wnm", weighted, vectors, preferred_element_type=jnp.float32
    )
    operator = lax.psum(local_operator, "vec").astype(jnp.bfloat16)
    running = walkers.astype(jnp.float32)
    folder = partial(fold_rows, operator)
    operand = walkers
    for degree in range(1, ORDER + 1):
        initial = jnp.zeros(running.shape, jnp.float32)
        summed = folder(initial, lax.all_gather(operand, "orb", axis=1, tiled=True), jnp.int32(0))
        new_term = (summed / degree).astype(jnp.bfloat16)
        running = running + new_term.astype(jnp.float32)
        if degree < ORDER:
            operand = new_term
    propagated = running.astype(jnp.bfloat16)
    every_walker = lax.all_gather(propagated, "walk", axis=0, tiled=True)
    every_log = lax.all_gather(new_log, "walk", axis=0, tiled=True)
    return (every_walker[copy_list], every_log[copy_list])


def solution(mesh):
    return jax.shard_map(
        per_device,
        mesh=mesh,
        in_specs=(
            P(("grp", "walk"), "orb", None),
            P(("grp", "walk"), None, None),
            P(),
            P("vec", "orb", None),
            P(("grp", "walk"), "vec"),
            P(("grp", "walk")),
            P(("grp", "walk")),
        ),
        out_specs=(P(("grp", "walk"), "orb", None), P(("grp", "walk"))),
        check_vma=False,
    )
```

profile of v0, /device:TPU:0, one launch (start us, length us, event | category | flops | bytes accessed | tf_op | source)
XLA Modules:
  0.0 276.8 jit_solution(15812537913773210420)
XLA Ops:
  7.2 0.0 copy-start
  7.2 0.0 copy-start.3
  7.2 0.0 all-gather.8.cloned.1.call-start
  7.2 0.7 all-gather.8.cloned.1.call-update
  7.9 0.0 all-gather.10.cloned.1.call-start
  8.0 1.4 convolution_convert_fusion.1
  9.4 0.4 copy.23
  9.8 0.0 copy-done
  9.8 0.0 copy-done.3
  9.8 0.0 copy-start.4
  9.8 1.5 convolution_convert_fusion.2
  11.3 1.4 copy.24
  12.7 0.4 convolution_bitcast_fusion
  13.2 2.6 psum.21
  15.8 0.0 copy-done.4
  15.8 3.3 %fusion = f32[8,256,512]{2,0,1:T(8,128)} fusion(bf16[8,256,512]{2,1,0:T(8,128)(2,1)S(1)} %copy-done, f32[8,8]{1,0:T(8,128)S(1)} %copy-done.4, f32[8,8]{1,0:T(8,128)S(1)} %psum.21), kind=kOutput, calls=%fused_computation.2 | convolution fusion | flops 16777472 | bytes 6291968 | tf_op jit(solution)/shard_map/wg,gnm->wnm/dot_general | solution.py:30
  19.1 0.1 subtract_reduce_fusion
  19.2 150.7 %all-reduce.3 = (bf16[8,256,512]{2,0,1:T(8,128)(2,1)}, f32[8]{0:T(128)S(1)}) all-reduce(f32[8,256,512]{2,0,1:T(8,128)} %fusion, f32[8]{0:T(128)S(1)} %subtract_reduce_fusion), channel_id=1, replica_groups=mesh['grp'=2,'vec'=4,'walk'=2,'orb'=2] {'vec'}, use_global_device_ids=true, to_apply=%region_1.0 | all-reduce | flops 1048584 | bytes 6291520 | tf_op jit(solution)/shard_map/psum | solution.py:33
  169.9 0.0 all-gather.8.cloned.1.call-done
  169.9 4.0 %convolution_convert_fusion = bf16[8,256,128]{2,1,0:T(8,128)(2,1)} fusion(bf16[8,512,128]{2,1,0:T(8,128)(2,1)} %all-gather.8.cloned.1.call-done, bf16[8,256,512]{2,0,1:T(8,128)(2,1)} %get-tuple-element.2), kind=kOutput, calls=%fused_computation.9 | convolution fusion | flops 268697600 | bytes 3670016 | tf_op jit(solution)/shard_map/wnm,wme->wne/dot_general | solution.py:13
  173.9 0.0 all-gather.10.cloned.1.call-update
  173.9 0.0 all-gather.12.cloned.1.call-start
  173.9 8.3 %all-gather.10.cloned.1.call-done = bf16[8,512,128]{2,1,0:T(8,128)(2,1)} async-done(((bf16[8,256,128]{2,1,0:T(8,128)(2,1)}), bf16[8,512,128]{2,1,0:T(8,128)(2,1)}) %all-gather.10.cloned.1.call-update) | async-done | bytes 1048592 | tf_op jit(solution)/shard_map/all_gather | solution.py:39
  182.2 4.1 %fusion.2 = bf16[8,256,128]{2,1,0:T(8,128)(2,1)} fusion(bf16[8,512,128]{2,1,0:T(8,128)(2,1)} %all-gather.10.cloned.1.call-done, bf16[8,256,512]{2,0,1:T(8,128)(2,1)} %get-tuple-element.2), kind=kOutput, calls=%fused_computation.11 | convolution fusion | flops 268959744 | bytes 3670016 | tf_op jit(solution)/shard_map/wnm,wme->wne/dot_general | solution.py:13
  186.3 0.0 all-gather.12.cloned.1.call-update
  186.3 0.0 all-gather.14.cloned.1.call-start
  186.4 10.3 %all-gather.12.cloned.1.call-done = bf16[8,512,128]{2,1,0:T(8,128)(2,1)} async-done(((bf16[8,256,128]{2,1,0:T(8,128)(2,1)}), bf16[8,512,128]{2,1,0:T(8,128)(2,1)}) %all-gather.12.cloned.1.call-update) | async-done | bytes 1048592 | tf_op jit(solution)/shard_map/all_gather | solution.py:39
  196.7 4.1 %fusion.3 = bf16[8,256,128]{2,1,0:T(8,128)(2,1)} fusion(bf16[8,512,128]{2,1,0:T(8,128)(2,1)} %all-gather.12.cloned.1.call-done, bf16[8,256,512]{2,0,1:T(8,128)(2,1)} %get-tuple-element.2), kind=kOutput, calls=%fused_computation.12 | convolution fusion | flops 268959744 | bytes 3670016 | tf_op jit(solution)/shard_map/wnm,wme->wne/dot_general | solution.py:13
  200.7 0.0 all-gather.14.cloned.1.call-update
  200.7 0.0 all-gather.16.cloned.1.call-start
  200.8 10.3 %all-gather.14.cloned.1.call-done = bf16[8,512,128]{2,1,0:T(8,128)(2,1)} async-done(((bf16[8,256,128]{2,1,0:T(8,128)(2,1)}), bf16[8,512,128]{2,1,0:T(8,128)(2,1)}) %all-gather.14.cloned.1.call-update) | async-done | bytes 1048592 | tf_op jit(solution)/shard_map/all_gather | solution.py:39
  211.1 4.0 %fusion.4 = bf16[8,256,128]{2,1,0:T(8,128)(2,1)} fusion(bf16[8,512,128]{2,1,0:T(8,128)(2,1)} %all-gather.14.cloned.1.call-done, bf16[8,256,512]{2,0,1:T(8,128)(2,1)} %get-tuple-element.2), kind=kOutput, calls=%fused_computation.13 | convolution fusion | flops 268959744 | bytes 3670016 | tf_op jit(solution)/shard_map/wnm,wme->wne/dot_general | solution.py:13
  215.1 0.0 all-gather.16.cloned.1.call-update
  215.2 0.0 copy-start.1
  215.2 0.0 copy-start.2
  215.2 0.0 all-gather.18.cloned.1.call-start
  215.2 10.3 %all-gather.16.cloned.1.call-done = bf16[8,512,128]{2,1,0:T(8,128)(2,1)} async-done(((bf16[8,256,128]{2,1,0:T(8,128)(2,1)}), bf16[8,512,128]{2,1,0:T(8,128)(2,1)}) %all-gather.16.cloned.1.call-update) | async-done | bytes 1048592 | tf_op jit(solution)/shard_map/all_gather | solution.py:39
  225.5 4.0 %fusion.5 = bf16[8,256,128]{2,1,0:T(8,128)(2,1)} fusion(bf16[8,512,128]{2,1,0:T(8,128)(2,1)} %all-gather.16.cloned.1.call-done, bf16[8,256,512]{2,0,1:T(8,128)(2,1)} %get-tuple-element.2), kind=kOutput, calls=%fused_computation.14 | convolution fusion | flops 268959744 | bytes 3670016 | tf_op jit(solution)/shard_map/wnm,wme->wne/dot_general | solution.py:13
  229.6 0.0 all-gather.18.cloned.1.call-update
  229.6 0.0 copy-start.7
  229.6 0.0 copy-start.5
  229.6 0.0 copy-start.6
  229.6 0.0 all-gather.20.cloned.1.call-start
  229.7 10.3 %all-gather.18.cloned.1.call-done = bf16[8,512,128]{2,1,0:T(8,128)(2,1)} async-done(((bf16[8,256,128]{2,1,0:T(8,128)(2,1)}), bf16[8,512,128]{2,1,0:T(8,128)(2,1)}) %all-gather.18.cloned.1.call-update) | async-done | bytes 1048592 | tf_op jit(solution)/shard_map/all_gather | solution.py:39
  239.9 0.0 copy-done.1
  239.9 0.0 copy-done.2
  239.9 4.7 %fusion.9 = bf16[8,256,128]{2,1,0:T(8,128)(2,1)} fusion(bf16[8,512,128]{2,1,0:T(8,128)(2,1)} %all-gather.18.cloned.1.call-done, bf16[8,256,128]{2,1,0:T(8,128)(2,1)} %fusion.5, bf16[8,256,128]{2,1,0:T(8,128)(2,1)} %fusion.4, bf16[8,256,128]{2,1,0:T(8,128)(2,1)} %fusion.3, bf16[8,256,128]{2,1,0:T(8,128)(2,1)} %fusion.2, ...), kind=kOutput, calls=%fused_computation.18 | convolution fusion | flops 272629760 | bytes 6815744 | tf_op jit(solution)/shard_map/wnm,wme->wne/dot_general | solution.py:13
  244.7 0.0 all-gather.20.cloned.1.call-update
  244.7 0.0 copy-done.7
  244.7 0.6 dynamic-slice
  246.0 0.0 copy-done.5
  246.0 0.1 add_dynamic-update-slice_fusion
  246.1 4.9 %all-reduce = f32[16]{0:T(128)S(1)} all-reduce(f32[16]{0:T(128)S(1)} %add_dynamic-update-slice_fusion), channel_id=1, replica_groups=mesh['grp'=2,'vec'=4,'walk'=2,'orb'=2] {'walk'}, use_global_device_ids=true, to_apply=%add | all-reduce | flops 16 | bytes 128
  251.0 0.0 copy-done.6
  251.0 1.2 gather_fusion.1
  252.2 15.2 %all-gather.20.cloned.1.call-done = bf16[16,256,128]{2,1,0:T(8,128)(2,1)} async-done(((bf16[8,256,128]{2,1,0:T(8,128)(2,1)}), bf16[16,256,128]{2,1,0:T(8,128)(2,1)}) %all-gather.20.cloned.1.call-update) | async-done | bytes 1048592 | tf_op jit(solution)/shard_map/all_gather | solution.py:45
  267.3 2.6 gather_fusion
  (3 shorter events, 0.0 us)
Async XLA Ops:
  7.2 2.6 copy-start
  7.2 2.6 copy-start.3
  7.2 162.7 %all-gather.8.cloned.1.call-start = ((), (), s32[]{:S(2)}) async-start(), calls=%async_computation | async-start | bytes 1572864 | tf_op jit(solution)/shard_map/all_gather | solution.py:39
  7.9 174.3 %all-gather.10.cloned.1.call-start = ((), (), s32[]{:S(2)}) async-start(), calls=%async_computation.1 | async-start | bytes 1572864 | tf_op jit(solution)/shard_map/all_gather | solution.py:39
  9.8 6.0 %copy-start.4 = (f32[8,8]{1,0:T(8,128)S(1)}, f32[8,8]{1,0:T(8,128)}, u32[]{:S(2)}) copy-start(f32[8,8]{1,0:T(8,128)} %param.11) | copy-start | bytes 772
  173.9 22.8 %all-gather.12.cloned.1.call-start = ((), (), s32[]{:S(2)}) async-start(), calls=%async_computation.2 | async-start | bytes 1572864 | tf_op jit(solution)/shard_map/all_gather | solution.py:39
  186.3 24.8 %all-gather.14.cloned.1.call-start = ((), (), s32[]{:S(2)}) async-start(), calls=%async_computation.3 | async-start | bytes 1572864 | tf_op jit(solution)/shard_map/all_gather | solution.py:39
  200.7 24.8 %all-gather.16.cloned.1.call-start = ((), (), s32[]{:S(2)}) async-start(), calls=%async_computation.4 | async-start | bytes 1572864 | tf_op jit(solution)/shard_map/all_gather | solution.py:39
  215.2 24.8 %copy-start.1 = (bf16[8,256,128]{2,1,0:T(8,128)(2,1)S(1)}, bf16[8,256,128]{2,1,0:T(8,128)(2,1)}, u32[]{:S(2)}) copy-start(bf16[8,256,128]{2,1,0:T(8,128)(2,1)} %param.7) | copy-start | bytes 1572868
  215.2 24.8 %copy-start.2 = (bf16[8,256,128]{2,1,0:T(8,128)(2,1)S(1)}, bf16[8,256,128]{2,1,0:T(8,128)(2,1)}, u32[]{:S(2)}) copy-start(bf16[8,256,128]{2,1,0:T(8,128)(2,1)} %convolution_convert_fusion) | copy-start | bytes 1572868
  215.2 24.8 %all-gather.18.cloned.1.call-start = ((), (), s32[]{:S(2)}) async-start(), calls=%async_computation.5 | async-start | bytes 1572864 | tf_op jit(solution)/shard_map/all_gather | solution.py:39
  229.6 15.1 %copy-start.7 = (u32[32]{0:T(128)S(1)}, u32[32]{0:T(128)}, u32[]{:S(2)}) copy-start(u32[32]{0:T(128)} %constant.31) | copy-start | bytes 388
  229.6 16.4 %copy-start.5 = (f32[8]{0:T(128)S(1)}, f32[8]{0:T(128)}, u32[]{:S(2)}) copy-start(f32[8]{0:T(128)} %param.12) | copy-start | bytes 100
  229.6 21.4 %copy-start.6 = (s32[8]{0:T(128)S(1)}, s32[8]{0:T(128)}, u32[]{:S(2)}) copy-start(s32[8]{0:T(128)} %param.13) | copy-start | bytes 100
  229.6 37.7 %all-gather.20.cloned.1.call-start = ((), (), s32[]{:S(2)}) async-start(), calls=%async_computation.6 | async-start | bytes 1572864 | tf_op jit(solution)/shard_map/all_gather | solution.py:45
Sparse Core Ops, SparseCore 0:
  9.5 11.7 all-gather.7
  174.0 8.1 all-gather.9
  186.4 10.1 all-gather.11
  200.9 10.1 all-gather.13
  215.3 10.1 all-gather.15
  229.7 10.1 all-gather.17
  244.8 22.4 all-gather.19
where the time goes:
time: 277 us
  blocking collectives  158 us (57%)
  waiting for transfers between devices  65.4 us (24%)
  matrix products  31.5 us (11%)
  between operations  14.9 us (5%)
  local copies, waits for them, and re-layouts  6.25 us (2%)
    psum x1, blocking collectives, per_device(): operator = lax.psum(local_operator, 'vec').astype(jnp.bfloat16)  151 us
    all_gather x6, waiting for transfers between devices, per_device(): lax.all_gather(operand, 'orb', axis=1, tiled=True)  49.4 us
    dot_general x6, matrix products, fold_rows(): jnp.einsum('wnm,wme->wne', operator, piece, preferred_element_type=jnp.fl...  24.9 us
    all_gather x1, waiting for transfers between devices, per_device(): every_walker = lax.all_gather(propagated, 'walk', axis=0, tiled=True)  15.2 us
  transfers between devices with their start and end apart: 7, of which 6 were waited for; matrix products, arithmetic and copies ran while one was open for 4% of the time, Pallas kernels for 0%

commit v1 on v0

--- a/solution.py
+++ b/solution.py
@@ -36,7 +36,13 @@
     operand = walkers
     for degree in range(1, ORDER + 1):
         initial = jnp.zeros(running.shape, jnp.float32)
-        summed = folder(initial, lax.all_gather(operand, "orb", axis=1, tiled=True), jnp.int32(0))
+        summed = folder(
+            initial,
+            jnp.concatenate(
+                lax.all_to_all(jnp.stack([operand] * lax.axis_size("orb")), "orb", 0, 0), axis=1
+            ),
+            jnp.int32(0),
+        )
         new_term = (summed / degree).astype(jnp.bfloat16)
         running = running + new_term.astype(jnp.float32)
         if degree < ORDER:

time: 277 us -> 248 us (0.90)
  waiting for transfers between devices: 65.4 us -> 12.2 us
  blocking collectives: 158 us -> 183 us
  matrix products: 31.5 us -> 19.7 us
  local copies, waits for them, and re-layouts: 6.25 us -> 10.3 us
  starting transfers between devices: 0.29 us -> 3.75 us
  other arithmetic: 0.23 us -> 3.1 us
    all_gather x6 -> x0, waiting for transfers between devices: 49.4 us -> none  [per_device(): lax.all_gather(operand, 'orb', axis=1, tiled=True)]
    all_to_all x0 -> x5, blocking collectives: none -> 23.1 us  [per_device(): lax.all_to_all(jnp.stack([operand] * lax.axis_size('orb')), 'orb', 0, 0)]
    dot_general x6, matrix products: 24.9 us -> 11.2 us  [fold_rows(): jnp.einsum('wnm,wme->wne', operator, piece, preferred_element_type=jnp.fl...]
    all_to_all x0 -> x1, starting transfers between devices: none -> 3.71 us  [per_device(): lax.all_to_all(jnp.stack([operand] * lax.axis_size('orb')), 'orb', 0, 0)]
    all_gather x1, waiting for transfers between devices: 15.2 us -> 12.2 us  [per_device(): every_walker = lax.all_gather(propagated, 'walk', axis=0, tiled=True)]
    another operation x0 -> x6, other arithmetic: none -> 2.87 us  [per_device(): jnp.stack([operand] * lax.axis_size('orb'))]
  transfers between devices with their start and end apart: 7 -> 2, of which waited for: 6 -> 1; matrix products, arithmetic and copies ran while one was open for 4% -> 6% of each run, Pallas kernels for 0% -> 0%
where the time goes in v1:
time: 248 us; the launch traced here: 247 us
  blocking collectives  183 us (74%)
  matrix products  19.7 us (8%)
  between operations  14.9 us (6%)
  waiting for transfers between devices  12.2 us (5%)
  local copies, waits for them, and re-layouts  10.3 us (4%)
  starting transfers between devices  3.75 us (2%)
  other arithmetic  3.1 us (1%)
    psum x1, blocking collectives, per_device(): operator = lax.psum(local_operator, 'vec').astype(jnp.bfloat16)  152 us
    all_to_all x5, blocking collectives, per_device(): lax.all_to_all(jnp.stack([operand] * lax.axis_size('orb')), 'orb', 0, 0)  23.1 us
    all_gather x1, waiting for transfers between devices, per_device(): every_walker = lax.all_gather(propagated, 'walk', axis=0, tiled=True)  12.2 us
    dot_general x6, matrix products, fold_rows(): jnp.einsum('wnm,wme->wne', operator, piece, preferred_element_type=jnp.fl...  11.2 us
  transfers between devices with their start and end apart: 2, of which 1 were waited for; matrix products, arithmetic and copies ran while one was open for 6% of the time, Pallas kernels for 0%

profile of v1, /device:TPU:0, one launch (start us, length us, event | category | flops | bytes accessed | tf_op | source)
XLA Modules:
  0.0 246.9 jit_solution(15519430494715761669)
XLA Ops:
  7.2 0.0 copy-start
  7.2 0.0 copy-start.3
  7.2 2.4 pad_maximum_fusion
  9.6 0.0 copy-start.4
  9.6 3.7 %all-to-all-start = ((bf16[2,8,256,128]{3,2,1,0:T(8,128)(2,1)}), bf16[2,8,256,128]{3,2,1,0:T(8,128)(2,1)S(1)}, u32[]{:S(2)}, u32[]{:S(2)}) async-start(bf16[2,8,256,128]{3,2,1,0:T(8,128)(2,1)} %pad_maximum_fusion), calls=%async_computation | async-start | bytes 2097152 | tf_op jit(solution)/shard_map/all_to_all | solution.py:42
  13.3 0.0 all-gather.2.cloned.1.call-start
  13.4 0.0 copy-done.3
  13.4 2.1 convolution_convert_fusion.1
  15.5 2.2 copy.30
  17.8 0.0 copy-done
  17.8 0.0 copy-done.4
  17.8 0.0 copy-start.5
  17.8 1.5 convolution_convert_fusion.2
  19.3 2.2 copy.31
  21.5 1.6 convolution_bitcast_fusion
  23.1 2.6 %psum.21 = f32[8,8]{1,0:T(8,128)S(1)} all-reduce(f32[8,8]{1,0:T(8,128)S(1)} %convolution_bitcast_fusion), channel_id=1, replica_groups=mesh['grp'=2,'vec'=4,'walk'=2,'orb'=2] {'orb'}, use_global_device_ids=true, to_apply=%region_0.0 | all-reduce | flops 64 | bytes 512 | tf_op jit(solution)/shard_map/psum | solution.py:24
  25.7 0.0 copy-done.5
  25.7 3.2 %fusion = f32[8,256,512]{2,0,1:T(8,128)} fusion(bf16[8,256,512]{2,1,0:T(8,128)(2,1)S(1)} %copy-done, f32[8,8]{1,0:T(8,128)S(1)} %copy-done.5, f32[8,8]{1,0:T(8,128)S(1)} %psum.21), kind=kOutput, calls=%fused_computation.2 | convolution fusion | flops 16777472 | bytes 6291968 | tf_op jit(solution)/shard_map/wg,gnm->wnm/dot_general | solution.py:30
  29.0 0.1 subtract_reduce_fusion
  29.1 0.0 all-to-all-done
  29.1 1.1 copy.33
  30.2 0.0 copy-start.2
  30.2 152.2 %all-reduce.3 = (bf16[8,256,512]{2,0,1:T(8,128)(2,1)}, f32[8]{0:T(128)S(1)}) all-reduce(f32[8,256,512]{2,0,1:T(8,128)} %fusion, f32[8]{0:T(128)S(1)} %subtract_reduce_fusion), channel_id=1, replica_groups=mesh['grp'=2,'vec'=4,'walk'=2,'orb'=2] {'vec'}, use_global_device_ids=true, to_apply=%region_1.0 | all-reduce | flops 1048584 | bytes 6291520 | tf_op jit(solution)/shard_map/psum | solution.py:33
  182.4 0.0 copy-done.2
  182.4 2.9 %convolution_convert_fusion = bf16[8,256,128]{2,1,0:T(8,128)(2,1)S(1)} fusion(bf16[8,512,128]{2,1,0:T(8,128)(2,1)S(1)} %bitcast.46, bf16[8,256,512]{2,0,1:T(8,128)(2,1)} %get-tuple-element.2), kind=kOutput, calls=%fused_computation.9 | convolution fusion | flops 268697600 | bytes 3670016 | tf_op jit(solution)/shard_map/wnm,wme->wne/dot_general | solution.py:13
  185.3 0.1 pad_maximum_fusion.1
  185.4 0.0 copy-start.7
  185.4 4.7 %all_to_all.30 = bf16[2,8,256,128]{3,2,1,0:T(8,128)(2,1)S(1)} all-to-all(bf16[2,8,256,128]{3,2,1,0:T(8,128)(2,1)S(1)} %pad_maximum_fusion.1), channel_id=1, replica_groups=mesh['grp'=2,'vec'=4,'walk'=2,'orb'=2] {'orb'}, dimensions={0} | all-to-all | bytes 2097152 | tf_op jit(solution)/shard_map/all_to_all | solution.py:42
  190.1 0.1 copy.35
  190.2 0.0 copy-done.7
  190.2 1.5 fusion.2
  191.7 0.1 pad_maximum_fusion.2
  191.8 4.6 %all_to_all.31 = bf16[2,8,256,128]{3,2,1,0:T(8,128)(2,1)S(1)} all-to-all(bf16[2,8,256,128]{3,2,1,0:T(8,128)(2,1)S(1)} %pad_maximum_fusion.2), channel_id=1, replica_groups=mesh['grp'=2,'vec'=4,'walk'=2,'orb'=2] {'orb'}, dimensions={0} | all-to-all | bytes 2097152 | tf_op jit(solution)/shard_map/all_to_all | solution.py:42
  196.4 0.1 copy.37
  196.5 1.5 fusion.3
  198.0 0.1 pad_maximum_fusion.3
  198.1 4.6 %all_to_all.32 = bf16[2,8,256,128]{3,2,1,0:T(8,128)(2,1)S(1)} all-to-all(bf16[2,8,256,128]{3,2,1,0:T(8,128)(2,1)S(1)} %pad_maximum_fusion.3), channel_id=1, replica_groups=mesh['grp'=2,'vec'=4,'walk'=2,'orb'=2] {'orb'}, dimensions={0} | all-to-all | bytes 2097152 | tf_op jit(solution)/shard_map/all_to_all | solution.py:42
  202.6 0.1 copy.39
  202.7 1.5 fusion.4
  204.2 0.1 pad_maximum_fusion.4
  204.3 4.6 %all_to_all.33 = bf16[2,8,256,128]{3,2,1,0:T(8,128)(2,1)S(1)} all-to-all(bf16[2,8,256,128]{3,2,1,0:T(8,128)(2,1)S(1)} %pad_maximum_fusion.4), channel_id=1, replica_groups=mesh['grp'=2,'vec'=4,'walk'=2,'orb'=2] {'orb'}, dimensions={0} | all-to-all | bytes 2097152 | tf_op jit(solution)/shard_map/all_to_all | solution.py:42
  208.9 0.1 copy.41
  209.0 1.5 fusion.5
  210.5 0.1 pad_maximum_fusion.5
  210.6 0.0 copy-start.1
  210.6 4.7 %all_to_all.34 = bf16[2,8,256,128]{3,2,1,0:T(8,128)(2,1)S(1)} all-to-all(bf16[2,8,256,128]{3,2,1,0:T(8,128)(2,1)S(1)} %pad_maximum_fusion.5), channel_id=1, replica_groups=mesh['grp'=2,'vec'=4,'walk'=2,'orb'=2] {'orb'}, dimensions={0} | all-to-all | bytes 2097152 | tf_op jit(solution)/shard_map/all_to_all | solution.py:42
  215.3 0.1 copy.43
  215.4 0.0 copy-done.1
  215.4 0.0 copy-start.9
  215.4 0.0 copy-start.6
  215.4 0.0 copy-start.8
  215.4 2.3 fusion.9
  217.7 0.0 all-gather.2.cloned.1.call-update
  217.7 0.0 copy-done.9
  217.7 0.6 dynamic-slice
  219.0 0.0 copy-done.6
  219.0 0.1 add_dynamic-update-slice_fusion
  219.1 4.9 %all-reduce = f32[16]{0:T(128)S(1)} all-reduce(f32[16]{0:T(128)S(1)} %add_dynamic-update-slice_fusion), channel_id=1, replica_groups=mesh['grp'=2,'vec'=4,'walk'=2,'orb'=2] {'walk'}, use_global_device_ids=true, to_apply=%add | all-reduce | flops 16 | bytes 128
  224.0 0.0 copy-done.8
  224.0 1.2 gather_fusion.1
  225.2 12.2 %all-gather.2.cloned.1.call-done = bf16[16,256,128]{2,1,0:T(8,128)(2,1)} async-done(((bf16[8,256,128]{2,1,0:T(8,128)(2,1)}), bf16[16,256,128]{2,1,0:T(8,128)(2,1)}) %all-gather.2.cloned.1.call-update) | async-done | bytes 1048592 | tf_op jit(solution)/shard_map/all_gather | solution.py:51
  237.4 2.6 %gather_fusion = bf16[8,256,128]{2,1,0:T(8,128)(2,1)} fusion(bf16[16,256,128]{2,1,0:T(8,128)(2,1)} %all-gather.2.cloned.1.call-done, s32[1024]{0:T(1024)S(1)} %pad_clamp_fusion), kind=kCustom, calls=%fused_computation | custom fusion | bytes 1048608 | tf_op jit(solution)/shard_map/gather | solution.py:53
  (3 shorter events, 0.0 us)
Async XLA Ops:
  7.2 10.6 %copy-start = (bf16[8,256,512]{2,1,0:T(8,128)(2,1)S(1)}, bf16[8,256,512]{2,1,0:T(8,128)(2,1)}, u32[]{:S(2)}) copy-start(bf16[8,256,512]{2,1,0:T(8,128)(2,1)} %param.10) | copy-start | bytes 6291460
  7.2 6.2 %copy-start.3 = (bf16[8,128,128]{2,1,0:T(8,128)(2,1)S(1)}, bf16[8,128,128]{2,1,0:T(8,128)(2,1)}, u32[]{:S(2)}) copy-start(bf16[8,128,128]{2,1,0:T(8,128)(2,1)} %param.8) | copy-start | bytes 786436
  9.6 8.1 %copy-start.4 = (bf16[512,128]{1,0:T(8,128)(2,1)S(1)}, bf16[512,128]{1,0:T(8,128)(2,1)}, u32[]{:S(2)}) copy-start(bf16[512,128]{1,0:T(8,128)(2,1)} %param.9) | copy-start | bytes 393220
  9.6 19.5 %all-to-all-start = ((bf16[2,8,256,128]{3,2,1,0:T(8,128)(2,1)}), bf16[2,8,256,128]{3,2,1,0:T(8,128)(2,1)S(1)}, u32[]{:S(2)}, u32[]{:S(2)}) async-start(bf16[2,8,256,128]{3,2,1,0:T(8,128)(2,1)} %pad_maximum_fusion), calls=%async_computation | async-start | bytes 2097152 | tf_op jit(solution)/shard_map/all_to_all | solution.py:42
  13.3 224.0 %all-gather.2.cloned.1.call-start = ((), (), s32[]{:S(2)}) async-start(), calls=%async_computation.6 | async-start | bytes 1572864 | tf_op jit(solution)/shard_map/all_gather | solution.py:51
  17.8 8.0 %copy-start.5 = (f32[8,8]{1,0:T(8,128)S(1)}, f32[8,8]{1,0:T(8,128)}, u32[]{:S(2)}) copy-start(f32[8,8]{1,0:T(8,128)} %param.11) | copy-start | bytes 772
  30.2 152.2 %copy-start.2 = (bf16[8,2,256,128]{3,2,1,0:T(8,128)(2,1)S(1)}, bf16[8,2,256,128]{3,2,1,0:T(8,128)(2,1)}, u32[]{:S(2)}) copy-start(bf16[8,2,256,128]{3,2,1,0:T(8,128)(2,1)} %copy.33) | copy-start | bytes 3145732
  185.4 4.8 %copy-start.7 = (bf16[8,256,512]{2,0,1:T(8,128)(2,1)S(1)}, bf16[8,256,512]{2,0,1:T(8,128)(2,1)}, u32[]{:S(2)}) copy-start(bf16[8,256,512]{2,0,1:T(8,128)(2,1)} %get-tuple-element.2) | copy-start | bytes 6291460
  210.6 4.8 %copy-start.1 = (bf16[8,256,128]{2,1,0:T(8,128)(2,1)S(1)}, bf16[8,256,128]{2,1,0:T(8,128)(2,1)}, u32[]{:S(2)}) copy-start(bf16[8,256,128]{2,1,0:T(8,128)(2,1)} %param.7) | copy-start | bytes 1572868
  215.4 2.3 copy-start.9
  215.4 3.6 %copy-start.6 = (f32[8]{0:T(128)S(1)}, f32[8]{0:T(128)}, u32[]{:S(2)}) copy-start(f32[8]{0:T(128)} %param.12) | copy-start | bytes 100
  215.4 8.6 %copy-start.8 = (s32[8]{0:T(128)S(1)}, s32[8]{0:T(128)}, u32[]{:S(2)}) copy-start(s32[8]{0:T(128)} %param.13) | copy-start | bytes 100
Sparse Core Ops, SparseCore 0:
  217.8 19.5 all-gather.1
